TPU v7x, 32 devices: a whole 2x2x4 slice. The times are simulated.
32 devices in a mesh: dp: 8 (over z, core), tensor: 4 (over y, x).
Axes of the slice: x: 2, y: 2, z: 4, core: 2. Of those that a mesh axis runs over, the one named last changes fastest.
Arguments:
- tokens_in: bfloat16 [1024, 8192], P(('dp', 'tensor')), may hold values from -6 to 6
- projector: bfloat16 [8192, 512], P('tensor'), may hold values from -0.0625 to 0.0625
- gate_pre: bfloat16 [1024, 15360], P('dp', 'tensor'), may hold values from -6 to 6
- up_pre: bfloat16 [1024, 15360], P('dp', 'tensor'), may hold values from -6 to 6
- hidden_grad: bfloat16 [1024, 15360], P('dp', 'tensor'), may hold values from -6 to 6
- moment_m: float32 [15360, 1024], P(('tensor', 'dp')), may hold values from -4 to 4
- moment_v: float32 [15360, 1024], P(('tensor', 'dp')), may hold values from 0.05 to 1
Outputs:
- m_next: float32 [15360, 1024], P(('tensor', 'dp'))
- v_next: float32 [15360, 1024], P(('tensor', 'dp'))
- direction: float32 [15360, 1024], P(('tensor', 'dp'))
All inputs are finite; a program needn't handle non-finite values.
Results may differ from a plain program's by a relative error of at most 0.00098.
Values may be sent and summed in bfloat16 or wider, within the bound.
A program may use at most 64 MiB of HBM per device.

v0:
```python
import functools

import jax
import jax.numpy as jnp
from jax import lax
from jax.experimental import pallas as pl
from jax.experimental.pallas import tpu as pltpu
from jax.sharding import PartitionSpec as P


MESH = pl.DeviceIdType.MESH
HELD = 5


def exchange_kernel(
    ndp, nt, tok_ref, prj_ref, gate_ref, up_ref, hg_ref, out_ref,
    g_v, u_v, h_v, prj_v, cols, part, rs_buf, xp_all, grads, recv,
    load_sem, tok_send, tok_recv, rs_send, rs_recv,
    xz_send, xt_send, xc_send, xp_recv, xc_recv, g_send, g_recv,
):
    d = lax.axis_index("dp")
    t = lax.axis_index("tensor")
    nz = ndp // 2
    z, c = d // 2, d % 2
    sub = tok_ref.shape[0]
    grp = sub * nt
    dcol = tok_ref.shape[1] // nt
    rows = recv.shape[2]
    rank = prj_ref.shape[1]
    half = ndp // 2
    half_tiles = half * rows // 128

    own_half = d // half
    inner = (z * (nz - 1 - z) + nz * nz - 1) // (nz * nz)
    first = own_half * (1 - inner) + (1 - own_half) * inner

    head = -(-rows // 128)
    spans = (
        (first * half_tiles, head),
        (first * half_tiles + head, half_tiles - head),
        ((1 - first) * half_tiles, half_tiles),
    )
    loads = []
    for i, (start, count) in enumerate(spans):
        at = pl.ds(pl.multiple_of(start * 128, 128), count * 128)
        for k, (src, dst) in enumerate(((gate_ref, g_v), (up_ref, u_v), (hg_ref, h_v))):
            loads.append(
                pltpu.make_async_copy(src.at[:, at], dst.at[:, at], load_sem.at[3 * i + k])
            )
    load_prj = pltpu.make_async_copy(prj_ref, prj_v, load_sem.at[9])
    own_tok = pltpu.make_async_copy(
        tok_ref.at[:, pl.ds(pl.multiple_of(t * dcol, 128), dcol)],
        cols.at[pl.ds(pl.multiple_of(t * sub, 16), sub), :],
        load_sem.at[10],
    )
    for load in loads[:3]:
        load.start()

    barrier = pltpu.get_barrier_semaphore()
    for k in range(1, ndp):
        pl.semaphore_signal(barrier, inc=1, device_id=((d + k) % ndp, t), device_id_type=MESH)
    for k in range(1, nt):
        pl.semaphore_signal(barrier, inc=1, device_id=(d, (t + k) % nt), device_id_type=MESH)

    for load in loads[3:]:
        load.start()
    load_prj.start()
    own_tok.start()

    def tok_copy(dest, src):
        return pltpu.make_async_remote_copy(
            src_ref=tok_ref.at[:, pl.ds(pl.multiple_of(dest * dcol, 128), dcol)],
            dst_ref=cols.at[pl.ds(pl.multiple_of(src * sub, 16), sub), :],
            send_sem=tok_send.at[dest],
            recv_sem=tok_recv.at[src],
            device_id=(d, dest),
            device_id_type=MESH,
        )

    def tile(i, carry):
        at = pl.ds(pl.multiple_of(i * 128, 128), 128)
        gate = g_v[:, at].astype(jnp.float32)
        upval = u_v[:, at].astype(jnp.float32)
        hgrad = h_v[:, at].astype(jnp.float32)
        sig = jax.nn.sigmoid(gate)
        grad_gate = hgrad * upval * sig * (1.0 + gate * (1.0 - sig))
        grad_up = hgrad * gate * sig
        grads[0, at, :] = grad_gate.astype(jnp.bfloat16).T
        grads[1, at, :] = grad_up.astype(jnp.bfloat16).T
        return carry

    def block_of(dest, side):
        return grads.at[side, pl.ds(pl.multiple_of(dest * rows, 16), rows), :]

    def grad_copy(dest, src, side):
        return pltpu.make_async_remote_copy(
            src_ref=block_of(dest, side),
            dst_ref=recv.at[src, side],
            send_sem=g_send.at[2 * dest + side],
            recv_sem=g_recv.at[2 * src + side],
            device_id=(dest, t),
            device_id_type=MESH,
        )

    def own_grad(side):
        return pltpu.make_async_copy(block_of(d, side), recv.at[d, side], load_sem.at[11 + side])

    def send_block(dest, side):
        @pl.when(dest != d)
        def _():
            grad_copy(dest, d, side).start()

        @pl.when(dest == d)
        def _():
            own_grad(side).start()

    def tiles_of(which, start, stop):
        lax.fori_loop(which * half_tiles + start, which * half_tiles + stop, tile, 0)

    for load in loads[:3]:
        load.wait()
    tiles_of(first, 0, head)
    pl.semaphore_wait(barrier, ndp + nt - 2)
    for k in range(1, nt):
        tok_copy((t + k) % nt, t).start()
    for side in (0, 1):
        send_block(first * half, side)

    for load in loads[3:6]:
        load.wait()
    done = head
    for j in range(1, half):
        need = -(-((j + 1) * rows) // 128)
        tiles_of(first, done, need)
        done = need
        for side in (0, 1):
            send = functools.partial(send_block, first * half + j, side)
            if 2 * j + side < HELD:
                send()
            else:
                pl.when(inner == 0)(send)
    for load in loads[6:]:
        load.wait()
    tiles_of(1 - first, 0, half_tiles)

    load_prj.wait()
    own_tok.wait()
    for k in range(1, nt):
        tok_copy(t, (t + k) % nt).wait_recv()
    part[...] = jnp.dot(cols[...], prj_v[...], preferred_element_type=jnp.float32)

    def rs_copy(dest, src):
        return pltpu.make_async_remote_copy(
            src_ref=part.at[pl.ds(pl.multiple_of(dest * sub, 16), sub), :],
            dst_ref=rs_buf.at[src],
            send_sem=rs_send.at[dest],
            recv_sem=rs_recv.at[src],
            device_id=(d, dest),
            device_id_type=MESH,
        )

    for k in range(1, nt):
        rs_copy((t + k) % nt, t).start()
    rs_buf[t] = part[pl.ds(pl.multiple_of(t * sub, 16), sub), :]
    for k in range(1, nt):
        rs_copy(t, (t + k) % nt).wait_recv()
    total = rs_buf[0]
    for k in range(1, nt):
        total = total + rs_buf[k]

    def piece(dd, tt):
        return xp_all.at[pl.ds(pl.multiple_of(dd * grp + tt * sub, 16), sub), :]

    xp_all[pl.ds(pl.multiple_of(d * grp + t * sub, 16), sub), :] = total.astype(jnp.bfloat16)

    def piece_copy(dd, tt, send_sem, dest):
        return pltpu.make_async_remote_copy(
            src_ref=piece(dd, tt),
            dst_ref=piece(dd, tt),
            send_sem=send_sem,
            recv_sem=xp_recv.at[dd * nt + tt],
            device_id=dest,
            device_id_type=MESH,
        )

    for k in range(1, nz):
        zz = (z + k) % nz
        piece_copy(d, t, xz_send.at[zz], (zz * 2 + c, t)).start()

    for j in range(half):
        for side in (0, 1):
            if 2 * j + side >= HELD:
                send = functools.partial(send_block, first * half + j, side)
                pl.when(inner == 1)(send)
    for j in range(half):
        for side in (0, 1):
            send_block((1 - first) * half + j, side)

    if nz == 4:
        order = [z, z + 1 - 2 * (z % 2), 3 - 3 * (z // 2), 2 - z // 2]
    else:
        order = [(z + k) % nz for k in range(nz)]

    for k, zz in enumerate(order):
        dd = zz * 2 + c
        if k:
            piece_copy(dd, t, xz_send.at[zz], (dd, t)).wait_recv()
        for kt in range(1, nt):
            tt = (t + kt) % nt
            piece_copy(dd, t, xt_send.at[zz * nt + tt], (d, tt)).start()

    partner = d + 1 - 2 * c

    def core_copy(zz, parity):
        group = xp_all.at[pl.ds(pl.multiple_of((zz * 2 + parity) * grp, 128), grp), :]
        return pltpu.make_async_remote_copy(
            src_ref=group,
            dst_ref=group,
            send_sem=xc_send.at[zz],
            recv_sem=xc_recv.at[zz],
            device_id=(partner, t),
            device_id_type=MESH,
        )

    for zz in order:
        for kt in range(1, nt):
            tt = (t + kt) % nt
            piece_copy(zz * 2 + c, tt, xt_send.at[zz * nt + tt], (d, tt)).wait_recv()
        core_copy(zz, c).start()

    for k, zz in enumerate(order):
        core_copy(zz, 1 - c).wait_recv()
        xp = xp_all[pl.ds(pl.multiple_of(zz * 2 * grp, 128), 2 * grp), :]
        for part_of in (0, 1):
            if k == 0:
                own_grad(part_of).wait()
                grad_copy(d, partner, part_of).wait_recv()
            else:
                grad_copy(d, zz * 2, part_of).wait_recv()
                grad_copy(d, zz * 2 + 1, part_of).wait_recv()
            lhs = jnp.concatenate([recv[zz * 2, part_of], recv[zz * 2 + 1, part_of]], axis=1)
            term = jnp.dot(lhs, xp, preferred_element_type=jnp.float32)
            at = slice(part_of * rank, (part_of + 1) * rank)
            if k == 0:
                out_ref[:, at] = term
            else:
                out_ref[:, at] += term

    for k in range(1, nt):
        dest = (t + k) % nt
        tok_copy(dest, t).wait_send()
        rs_copy(dest, t).wait_send()
        for zz in range(nz):
            piece_copy(zz * 2 + c, t, xt_send.at[zz * nt + dest], (d, dest)).wait_send()
    for k in range(1, nz):
        zz = (z + k) % nz
        piece_copy(d, t, xz_send.at[zz], (zz * 2 + c, t)).wait_send()
    for zz in range(nz):
        core_copy(zz, c).wait_send()
    for k in range(1, ndp):
        for side in (0, 1):
            grad_copy((d + k) % ndp, d, side).wait_send()


def exchange(ndp, nt, tokens_in, projector, gate_pre, up_pre, hidden_grad):
    sub, width = tokens_in.shape
    depth, rank = projector.shape
    grp, cols = gate_pre.shape
    rows = cols // ndp
    dma = pltpu.SemaphoreType.DMA
    bf, f32 = jnp.bfloat16, jnp.float32
    nz = ndp // 2
    operands = (tokens_in, projector, gate_pre, up_pre, hidden_grad)
    flops = 2 * grp * depth * rank + 4 * rows * grp * ndp * rank
    return pl.pallas_call(
        functools.partial(exchange_kernel, ndp, nt),
        out_shape=jax.ShapeDtypeStruct((rows, 2 * rank), f32),
        in_specs=[pl.BlockSpec(memory_space=pltpu.HBM)] * 5,
        out_specs=pl.BlockSpec(memory_space=pltpu.VMEM),
        scratch_shapes=[
            pltpu.VMEM((grp, cols), bf),
            pltpu.VMEM((grp, cols), bf),
            pltpu.VMEM((grp, cols), bf),
            pltpu.VMEM((depth, rank), bf),
            pltpu.VMEM((grp, depth), bf),
            pltpu.VMEM((grp, rank), f32),
            pltpu.VMEM((nt, sub, rank), f32),
            pltpu.VMEM((grp * ndp, rank), bf),
            pltpu.VMEM((2, cols, grp), bf),
            pltpu.VMEM((ndp, 2, rows, grp), bf),
            dma((13,)),
            dma((nt,)),
            dma((nt,)),
            dma((nt,)),
            dma((nt,)),
            dma((nz,)),
            dma((nz * nt,)),
            dma((nz,)),
            dma((ndp * nt,)),
            dma((nz,)),
            dma((2 * ndp,)),
            dma((2 * ndp,)),
        ],
        compiler_params=pltpu.CompilerParams(
            collective_id=0, has_side_effects=True, vmem_limit_bytes=32 * 1024 * 1024
        ),
        cost_estimate=pl.CostEstimate(
            flops=flops, bytes_accessed=8 * grp * cols, transcendentals=grp * cols
        ),
    )(*[pltpu.with_memory_space_constraint(x, pltpu.HBM) for x in operands])


def fits(ndp, nt, tokens_in, projector, gate_pre):
    sub, width = tokens_in.shape
    grp, cols = gate_pre.shape
    return (
        ndp % 2 == 0
        and ndp >= 4
        and nt >= 2
        and grp == 128
        and sub * nt == grp
        and sub % 16 == 0
        and cols % ndp == 0
        and (cols // ndp) % 16 == 0
        and cols % 256 == 0
        and width % (128 * nt) == 0
        and projector.shape[0] == width // nt
        and projector.shape[1] % 128 == 0
        and cols <= 8192
        and projector.size <= 2**21
        and grp * ndp <= 4096
    )


def finish(summed, total_tokens, moment_m, moment_v):
    proj = summed * float(total_tokens) ** (-0.5)
    m_next = 0.9 * moment_m + 0.1 * proj
    v_next = 0.95 * moment_v + 0.05 * proj * proj
    direction = m_next / (jnp.sqrt(v_next) + 1e-08)
    return (m_next, v_next, direction)


def finish_kernel(total_tokens, steps, sum_ref, m_ref, v_ref, *refs):
    outs, bufs, sem = refs[:3], refs[3:6], refs[6]
    rows = sum_ref.shape[0] // steps
    copies = []
    for i in range(steps):
        at = slice(i * rows, (i + 1) * rows)
        values = finish(sum_ref[at, :], total_tokens, m_ref[at, :], v_ref[at, :])
        for k in range(3):
            bufs[k][at, :] = values[k]
            copy = pltpu.make_async_copy(
                bufs[k].at[at, :], outs[k].at[at, :], sem.at[3 * i + k]
            )
            copy.start()
            copies.append(copy)
    for copy in copies:
        copy.wait()


def finish_call(summed, total_tokens, moment_m, moment_v):
    steps = 6
    shape = jax.ShapeDtypeStruct(summed.shape, jnp.float32)
    return pl.pallas_call(
        functools.partial(finish_kernel, total_tokens, steps),
        out_shape=(shape,) * 3,
        in_specs=[pl.BlockSpec(memory_space=pltpu.VMEM)] * 3,
        out_specs=[pl.BlockSpec(memory_space=pltpu.HBM)] * 3,
        scratch_shapes=[pltpu.VMEM(summed.shape, jnp.float32)] * 3
        + [pltpu.SemaphoreType.DMA((3 * steps,))],
        compiler_params=pltpu.CompilerParams(vmem_limit_bytes=16 * 1024 * 1024),
    )(summed, moment_m, moment_v)


def local(tokens_in, projector, gate_pre, up_pre, hidden_grad, moment_m, moment_v):
    ndp, nt = lax.axis_size("dp"), lax.axis_size("tensor")
    if fits(ndp, nt, tokens_in, projector, gate_pre):
        summed = exchange(ndp, nt, tokens_in, projector, gate_pre, up_pre, hidden_grad)
        return tuple(finish_call(summed, gate_pre.shape[0] * ndp, moment_m, moment_v))
    gate = gate_pre.astype(jnp.float32)
    hgrad = hidden_grad.astype(jnp.float32)
    sig = jax.nn.sigmoid(gate)
    upval = up_pre.astype(jnp.float32)
    grad_gate = (hgrad * upval * sig * (1.0 + gate * (1.0 - sig))).astype(jnp.bfloat16)
    grad_up = (hgrad * gate * sig).astype(jnp.bfloat16)
    grads = jnp.stack([grad_gate, grad_up])
    grads = lax.all_to_all(grads, "dp", split_axis=2, concat_axis=1, tiled=True)
    columns = lax.all_to_all(tokens_in, "tensor", split_axis=1, concat_axis=0, tiled=True)
    partial_xp = jnp.dot(columns, projector, preferred_element_type=jnp.float32)
    own_rows = lax.psum_scatter(partial_xp, "tensor", scatter_dimension=0, tiled=True).astype(
        jnp.bfloat16
    )
    xp = lax.all_gather(own_rows, ("dp", "tensor"), axis=0, tiled=True)
    contract = (((0,), (0,)), ((), ()))
    halves = [
        lax.dot_general(grads[k], xp, contract, preferred_element_type=jnp.float32) for k in (0, 1)
    ]
    summed = jnp.concatenate(halves, axis=1)
    return finish(summed, xp.shape[0], moment_m, moment_v)


def solution(mesh):
    return jax.shard_map(
        local,
        mesh=mesh,
        in_specs=(
            P(("dp", "tensor"), None),
            P("tensor", None),
            P("dp", "tensor"),
            P("dp", "tensor"),
            P("dp", "tensor"),
            P(("tensor", "dp"), None),
            P(("tensor", "dp"), None),
        ),
        out_specs=(P(("tensor", "dp"), None), P(("tensor", "dp"), None), P(("tensor", "dp"), None)),
        check_vma=False,
    )
```

profile of v0, /device:TPU:9, one launch (start us, length us, event | category | flops | bytes accessed | tf_op | source)
XLA Modules:
  0.0 54.4 jit_solution(10814501026351904075)
XLA Ops:
  0.6 0.0 copy-start.1
  0.6 0.0 copy-start
  0.7 50.9 %shard_map.94.sum_ref = f32[480,1024]{1,0:T(8,128)S(1)} custom-call(bf16[32,8192]{1,0:T(8,128)(2,1)} %tok_ref.1, bf16[2048,512]{1,0:T(8,128)(2,1)} %prj_ref.1, bf16[128,3840]{1,0:T(8,128)(2,1)} %gate_ref.1, bf16[128,3840]{1,0:T(8,128)(2,1)} %up_ref.1, bf16[128,3840]{1,0:T(8,128)(2,1)} %hg_ref.1), custom_call_target="tpu_custom_call" | custom-call | flops 1275068416 | bytes 3932160 | tf_op jit(solution)/shard_map/pallas_call | solution.py:275
  51.6 0.0 copy-done.1
  51.6 0.0 copy-done
  51.6 2.8 %shard_map.95 = (f32[480,1024]{1,0:T(8,128)}, f32[480,1024]{1,0:T(8,128)}, f32[480,1024]{1,0:T(8,128)}) custom-call(f32[480,1024]{1,0:T(8,128)S(1)} %shard_map.94.sum_ref, f32[480,1024]{1,0:T(8,128)S(1)} %copy-done, f32[480,1024]{1,0:T(8,128)S(1)} %copy-done.1), custom_call_target="tpu_custom_call" | custom-call | tf_op jit(solution)/shard_map/pallas_call | solution.py:364
Async XLA Ops:
  0.6 51.0 %copy-start.1 = (f32[480,1024]{1,0:T(8,128)S(1)}, f32[480,1024]{1,0:T(8,128)}, u32[]{:S(2)}) copy-start(f32[480,1024]{1,0:T(8,128)} %v_ref.1) | copy-start | bytes 5898244
  0.6 51.0 %copy-start = (f32[480,1024]{1,0:T(8,128)S(1)}, f32[480,1024]{1,0:T(8,128)}, u32[]{:S(2)}) copy-start(f32[480,1024]{1,0:T(8,128)} %m_ref.1) | copy-start | bytes 5898244
where the time goes:
time: 54.6 us; the launch traced here: 54.4 us
  Pallas kernels  53.7 us (98%)
  between operations  0.67 us (1%)
    pallas_call x1, Pallas kernels, exchange(): pl.pallas_call(functools.partial(exchange_kernel, ndp, nt), out_shape=jax...  50.9 us
    pallas_call x1, Pallas kernels, finish_call(): pl.pallas_call(functools.partial(finish_kernel, total_tokens, steps), out...  2.79 us

commit v1 on v0

v1 whole, which is shorter than its diff:
```python
import functools

import jax
import jax.numpy as jnp
from jax import lax
from jax.experimental import pallas as pl
from jax.experimental.pallas import tpu as pltpu
from jax.sharding import PartitionSpec as P


MESH = pl.DeviceIdType.MESH
TAILS = 3
OUTER_EARLY = ((1, 2, 0), (1, 0, 0), (0, 0, 1))
OUTER = ((1, 3, 0), (1, 1, 0), (0, 1, 1), (1, 2, 1), (1, 0, 1), (1, 3, 1), (1, 1, 1))
INNER_EARLY = ((0, 2, 0), (1, 0, 0), (1, 1, 0))
EARLY_CUTS = ((0, 0),)
INNER = ((0, 3, 0), (0, 2, 1), (0, 3, 1))
OWN = ((1, 0, 1), (1, 1, 1))
def pieces(rows):
    cuts = [-(-rows * i // (16 * TAILS)) * 16 for i in range(TAILS)] + [rows]
    return list(zip(cuts, cuts[1:]))


def exchange_kernel(
    ndp, nt, tok_ref, prj_ref, gate_ref, up_ref, hg_ref, out_ref,
    acts, prj_v, cols, part, rs_buf, xp_all, grads, recv,
    load_sem, tok_send, tok_recv, rs_send, rs_recv,
    xp_send, xz_recv, xt_recv, xc_recv, g_send, g_recv, cut_recv, late,
):
    d = lax.axis_index("dp")
    t = lax.axis_index("tensor")
    nz = ndp // 2
    z, c = d // 2, d % 2
    sub = tok_ref.shape[0]
    grp = sub * nt
    dcol = tok_ref.shape[1] // nt
    rows = recv.shape[2]
    rank = prj_ref.shape[1]
    half = ndp // 2
    half_tiles = half * rows // 128
    cut = pieces(rows)

    own_half = d // half
    inner = (z + 1) // 2 % 2
    up = z % 2
    adj = z + 1 - 2 * up
    far = (nz - 1) * (1 - z // 2)
    opp = 2 - z // 2
    first = own_half * (1 - inner) + (1 - own_half) * inner
    second = 1 - first

    def dest_of(which, j):
        return which * half + up * j + (1 - up) * (half - 1 - j)

    head = -(-rows // 128)
    spans = ((first, 0, head), (first, head, half_tiles), (second, 0, half_tiles))
    loads, places = [], []
    for i, (which, start, stop) in enumerate(spans):
        low = which * half_tiles + up * start + (1 - up) * (half_tiles - stop)
        at = pl.ds(pl.multiple_of(low * 128, 128), (stop - start) * 128)
        places.append(at)
        for k, src in enumerate((gate_ref, up_ref, hg_ref)):
            loads.append(pltpu.make_async_copy(src.at[:, at], acts.at[k, :, at], load_sem.at[i]))
    load_prj = pltpu.make_async_copy(prj_ref, prj_v, load_sem.at[3])
    own_tok = pltpu.make_async_copy(
        tok_ref.at[:, pl.ds(pl.multiple_of(t * dcol, 128), dcol)],
        cols.at[pl.ds(pl.multiple_of(t * sub, 16), sub), :],
        tok_recv.at[0],
    )
    for load in loads[:3]:
        load.start()

    def drain(ref, sem):
        pltpu.make_async_copy(ref, ref, sem).wait()

    barrier = pltpu.get_barrier_semaphore()

    def greet(dp, tensor):
        pl.semaphore_signal(barrier, inc=1, device_id=(dp, tensor), device_id_type=MESH)

    @pl.when(z < nz - 1)
    def _():
        for k in range(1, ndp):
            greet((d + k) % ndp, t)

    @pl.when(z == nz - 1)
    def _():
        greet(d + 1 - 2 * c, t)

    for k in range(1, nt):
        greet(d, (t + k) % nt)

    for load in loads[3:]:
        load.start()
    load_prj.start()
    own_tok.start()

    def tok_copy(dest, src):
        return pltpu.make_async_remote_copy(
            src_ref=tok_ref.at[:, pl.ds(pl.multiple_of(dest * dcol, 128), dcol)],
            dst_ref=cols.at[pl.ds(pl.multiple_of(src * sub, 16), sub), :],
            send_sem=tok_send.at[0],
            recv_sem=tok_recv.at[0],
            device_id=(d, dest),
            device_id_type=MESH,
        )

    def tile(i, carry):
        at = pl.ds(pl.multiple_of(i * 128, 128), 128)
        gate = acts[0, :, at].astype(jnp.float32)
        upval = acts[1, :, at].astype(jnp.float32)
        hgrad = acts[2, :, at].astype(jnp.float32)
        sig = jax.nn.sigmoid(gate)
        grad_gate = hgrad * upval * sig * (1.0 + gate * (1.0 - sig))
        grad_up = hgrad * gate * sig
        grads[0, at, :] = grad_gate.astype(jnp.bfloat16).T
        grads[1, at, :] = grad_up.astype(jnp.bfloat16).T
        return carry

    def tiles_of(which, start, stop):
        low = which * half_tiles + up * start + (1 - up) * (half_tiles - stop)
        lax.fori_loop(low, low + stop - start, tile, 0)

    def block_of(dest, side):
        return grads.at[side, pl.ds(pl.multiple_of(dest * rows, 16), rows), :]

    def grad_copy(dest, src, side):
        return pltpu.make_async_remote_copy(
            src_ref=block_of(dest, side),
            dst_ref=recv.at[src, side],
            send_sem=g_send.at[0],
            recv_sem=g_recv.at[src // 2 * 2 + side],
            device_id=(dest, t),
            device_id_type=MESH,
        )

    def cut_copy(dest, src, p):
        start, stop = cut[p]
        at = pl.ds(pl.multiple_of(dest * rows + start, 16), stop - start)
        return pltpu.make_async_remote_copy(
            src_ref=grads.at[1, at, :],
            dst_ref=recv.at[src, 1, start:stop, :],
            send_sem=g_send.at[0],
            recv_sem=cut_recv.at[p],
            device_id=(dest, t),
            device_id_type=MESH,
        )

    def own_grad(side):
        return pltpu.make_async_copy(block_of(d, side), recv.at[d, side], g_recv.at[2 * z + side])

    def send_near(dest, side):
        @pl.when(dest != d)
        def _():
            grad_copy(dest, d, side).start()

        @pl.when(dest == d)
        def _():
            own_grad(side).start()

    def send(which, j, side):
        grad_copy(dest_of(which, j), d, side).start()

    def send_all(plan):
        for part_of, j, side in plan:
            send((first, second)[part_of], j, side)

    def send_cuts(plan):
        for p, j in plan:
            cut_copy(dest_of(first, j), d, p).start()

    def need(j):
        return -(-((j + 1) * rows) // 128)

    drain(acts.at[:, :, places[0]], load_sem.at[0])
    tiles_of(first, 0, head)
    pl.semaphore_wait(barrier, nt - 1 + jnp.where(z == nz - 1, ndp - 1, ndp - 3))
    send(first, 0, 0)
    for k in range(1, nt):
        tok_copy((t + k) % nt, t).start()

    @pl.when(z == nz - 1)
    def _():
        for k in range(ndp - 2):
            pl.semaphore_signal(late, inc=1, device_id=(k, t), device_id_type=MESH)

    drain(acts.at[:, :, places[1]], load_sem.at[1])
    tiles_of(first, head, need(1))
    send(first, 1, 0)
    tiles_of(first, need(1), half_tiles)
    drain(acts.at[:, :, places[2]], load_sem.at[2])
    tiles_of(second, 0, half_tiles)

    @pl.when(z < nz - 1)
    def _():
        pl.semaphore_wait(late, 2)

    @pl.when(inner == 0)
    def _():
        send_all(OUTER_EARLY)

    @pl.when(inner == 1)
    def _():
        send_all(INNER_EARLY)
        send_cuts(EARLY_CUTS)

    for j in (2, 3):
        for side in (0, 1):
            send_near(dest_of(own_half, j), side)

    load_prj.wait()
    drain(cols, tok_recv.at[0])
    part[...] = jnp.dot(cols[...], prj_v[...], preferred_element_type=jnp.float32)

    def rs_copy(dest, src):
        return pltpu.make_async_remote_copy(
            src_ref=part.at[pl.ds(pl.multiple_of(dest * sub, 16), sub), :],
            dst_ref=rs_buf.at[src],
            send_sem=rs_send.at[0],
            recv_sem=rs_recv.at[0],
            device_id=(d, dest),
            device_id_type=MESH,
        )

    for k in range(1, nt):
        rs_copy((t + k) % nt, t).start()
    rs_buf[t] = part[pl.ds(pl.multiple_of(t * sub, 16), sub), :]
    drain(rs_buf.at[: nt - 1], rs_recv.at[0])
    total = rs_buf[0]
    for k in range(1, nt):
        total = total + rs_buf[k]

    def piece(dd, tt):
        return xp_all.at[pl.ds(pl.multiple_of(dd * grp + tt * sub, 16), sub), :]

    xp_all[pl.ds(pl.multiple_of(d * grp + t * sub, 16), sub), :] = total.astype(jnp.bfloat16)

    def piece_copy(dd, tt, recv_sem, dest):
        return pltpu.make_async_remote_copy(
            src_ref=piece(dd, tt),
            dst_ref=piece(dd, tt),
            send_sem=xp_send.at[0],
            recv_sem=recv_sem,
            device_id=dest,
            device_id_type=MESH,
        )

    def along_z(zz, dest):
        piece_copy(zz * 2 + c, t, xz_recv.at[zz], (dest * 2 + c, t)).start()

    along_z(z, opp)
    along_z(z, adj)

    @pl.when(inner == 0)
    def _():
        send_all(OUTER)

    @pl.when(inner == 1)
    def _():
        send_all(INNER)
        send_cuts([(p, j) for p in range(TAILS) for j in (0, 1) if (p, j) not in EARLY_CUTS])

    order = [z, adj, far, opp]

    for k, zz in enumerate(order):
        dd = zz * 2 + c
        if k:
            drain(piece(dd, t), xz_recv.at[zz])
        if k > 1:
            pl.when(inner == 1)(functools.partial(along_z, zz, adj))
        for kt in range(1, nt):
            piece_copy(dd, t, xt_recv.at[zz], (d, (t + kt) % nt)).start()

    @pl.when(inner == 1)
    def _():
        send_all(OWN)

    partner = d + 1 - 2 * c

    def core_copy(zz, parity):
        group = xp_all.at[pl.ds(pl.multiple_of((zz * 2 + parity) * grp, 128), grp), :]
        return pltpu.make_async_remote_copy(
            src_ref=group,
            dst_ref=group,
            send_sem=xp_send.at[0],
            recv_sem=xc_recv.at[zz],
            device_id=(partner, t),
            device_id_type=MESH,
        )

    for zz in order:
        drain(xp_all.at[: (nt - 1) * sub, :], xt_recv.at[zz])
        core_copy(zz, c).start()

    def add_term(k, zz, side, low, count):
        at = pl.ds(low, count)
        xp = xp_all[pl.ds(pl.multiple_of(zz * 2 * grp, 128), 2 * grp), :]
        lhs = jnp.concatenate([recv[zz * 2, side, at, :], recv[zz * 2 + 1, side, at, :]], axis=1)
        term = jnp.dot(lhs, xp, preferred_element_type=jnp.float32)
        cols_at = slice(side * rank, (side + 1) * rank)
        if k == 0:
            out_ref[at, cols_at] = term
        else:
            out_ref[at, cols_at] += term

    def take(k, zz, side):
        drain(recv.at[pl.ds(zz * 2, 2), side], g_recv.at[2 * zz + side])
        add_term(k, zz, side, 0, rows)

    for k in (0, 1):
        core_copy(order[k], 1 - c).wait_recv()
        for side in (0, 1):
            take(k, order[k], side)
    core_copy(far, 1 - c).wait_recv()
    core_copy(opp, 1 - c).wait_recv()
    drain(cols.at[: (nt - 1) * sub, :], tok_send.at[0])
    drain(rs_buf.at[: nt - 1], rs_send.at[0])
    moved = (nt - 1) * nz + nt * nz + 2
    pl.when(inner == 0)(lambda: drain(xp_all.at[: moved * sub, :], xp_send.at[0]))
    pl.when(inner == 1)(lambda: drain(xp_all.at[: (moved + 2) * sub, :], xp_send.at[0]))
    take(3, opp, 0)
    take(2, far, 0)
    take(2, far, 1)

    @pl.when(inner == 0)
    def _():
        take(3, opp, 1)

    @pl.when(inner == 1)
    def _():
        for p, (start, stop) in enumerate(cut):
            drain(recv.at[pl.ds(opp * 2, 2), 1, start:stop, :], cut_recv.at[p])
            add_term(3, opp, 1, start, stop - start)

    drain(recv.at[: ndp - 1], g_send.at[0])


def exchange(ndp, nt, tokens_in, projector, gate_pre, up_pre, hidden_grad):
    sub, width = tokens_in.shape
    depth, rank = projector.shape
    grp, cols = gate_pre.shape
    rows = cols // ndp
    dma = pltpu.SemaphoreType.DMA
    bf, f32 = jnp.bfloat16, jnp.float32
    nz = ndp // 2
    operands = (tokens_in, projector, gate_pre, up_pre, hidden_grad)
    flops = 2 * grp * depth * rank + 4 * rows * grp * ndp * rank
    return pl.pallas_call(
        functools.partial(exchange_kernel, ndp, nt),
        out_shape=jax.ShapeDtypeStruct((rows, 2 * rank), f32),
        in_specs=[pl.BlockSpec(memory_space=pltpu.HBM)] * 5,
        out_specs=pl.BlockSpec(memory_space=pltpu.VMEM),
        scratch_shapes=[
            pltpu.VMEM((3, grp, cols), bf),
            pltpu.VMEM((depth, rank), bf),
            pltpu.VMEM((grp, depth), bf),
            pltpu.VMEM((grp, rank), f32),
            pltpu.VMEM((nt, sub, rank), f32),
            pltpu.VMEM((grp * ndp, rank), bf),
            pltpu.VMEM((2, cols, grp), bf),
            pltpu.VMEM((ndp, 2, rows, grp), bf),
            dma((4,)),
            dma((1,)),
            dma((1,)),
            dma((1,)),
            dma((1,)),
            dma((1,)),
            dma((nz,)),
            dma((nz,)),
            dma((nz,)),
            dma((1,)),
            dma((2 * nz,)),
            dma((TAILS,)),
            pltpu.SemaphoreType.REGULAR,
        ],
        compiler_params=pltpu.CompilerParams(
            collective_id=0, has_side_effects=True, vmem_limit_bytes=32 * 1024 * 1024
        ),
        cost_estimate=pl.CostEstimate(
            flops=flops, bytes_accessed=8 * grp * cols, transcendentals=grp * cols
        ),
    )(*[pltpu.with_memory_space_constraint(x, pltpu.HBM) for x in operands])


def fits(ndp, nt, tokens_in, projector, gate_pre):
    sub, width = tokens_in.shape
    grp, cols = gate_pre.shape
    return (
        ndp == 8
        and nt >= 2
        and grp == 128
        and sub * nt == grp
        and sub % 16 == 0
        and cols % ndp == 0
        and (cols // ndp) % 16 == 0
        and cols // ndp >= 256
        and cols % 256 == 0
        and width % (128 * nt) == 0
        and projector.shape[0] == width // nt
        and projector.shape[1] % 128 == 0
        and cols <= 8192
        and projector.size <= 2**21
        and grp * ndp <= 4096
    )


def finish(summed, total_tokens, moment_m, moment_v):
    proj = summed * float(total_tokens) ** (-0.5)
    m_next = 0.9 * moment_m + 0.1 * proj
    v_next = 0.95 * moment_v + 0.05 * proj * proj
    direction = m_next / (jnp.sqrt(v_next) + 1e-08)
    return (m_next, v_next, direction)


def finish_kernel(total_tokens, steps, sum_ref, m_ref, v_ref, *refs):
    outs, bufs, sem = refs[:3], refs[3:6], refs[6]
    rows = sum_ref.shape[0] // steps
    for i in range(steps):
        at = slice(i * rows, (i + 1) * rows)
        values = finish(sum_ref[at, :], total_tokens, m_ref[at, :], v_ref[at, :])
        for k in range(3):
            bufs[k][at, :] = values[k]
            copy = pltpu.make_async_copy(
                bufs[k].at[at, :], outs[k].at[at, :], sem.at[k]
            )
            copy.start()
    for k in range(3):
        pltpu.make_async_copy(bufs[k], outs[k], sem.at[k]).wait()


def finish_call(summed, total_tokens, moment_m, moment_v):
    steps = 6
    shape = jax.ShapeDtypeStruct(summed.shape, jnp.float32)
    return pl.pallas_call(
        functools.partial(finish_kernel, total_tokens, steps),
        out_shape=(shape,) * 3,
        in_specs=[pl.BlockSpec(memory_space=pltpu.VMEM)] * 3,
        out_specs=[pl.BlockSpec(memory_space=pltpu.HBM)] * 3,
        scratch_shapes=[pltpu.VMEM(summed.shape, jnp.float32)] * 3
        + [pltpu.SemaphoreType.DMA((3,))],
        compiler_params=pltpu.CompilerParams(vmem_limit_bytes=16 * 1024 * 1024),
    )(summed, moment_m, moment_v)


def local(tokens_in, projector, gate_pre, up_pre, hidden_grad, moment_m, moment_v):
    ndp, nt = lax.axis_size("dp"), lax.axis_size("tensor")
    if fits(ndp, nt, tokens_in, projector, gate_pre):
        summed = exchange(ndp, nt, tokens_in, projector, gate_pre, up_pre, hidden_grad)
        return tuple(finish_call(summed, gate_pre.shape[0] * ndp, moment_m, moment_v))
    gate = gate_pre.astype(jnp.float32)
    hgrad = hidden_grad.astype(jnp.float32)
    sig = jax.nn.sigmoid(gate)
    upval = up_pre.astype(jnp.float32)
    grad_gate = (hgrad * upval * sig * (1.0 + gate * (1.0 - sig))).astype(jnp.bfloat16)
    grad_up = (hgrad * gate * sig).astype(jnp.bfloat16)
    grads = jnp.stack([grad_gate, grad_up])
    grads = lax.all_to_all(grads, "dp", split_axis=2, concat_axis=1, tiled=True)
    columns = lax.all_to_all(tokens_in, "tensor", split_axis=1, concat_axis=0, tiled=True)
    partial_xp = jnp.dot(columns, projector, preferred_element_type=jnp.float32)
    own_rows = lax.psum_scatter(partial_xp, "tensor", scatter_dimension=0, tiled=True).astype(
        jnp.bfloat16
    )
    xp = lax.all_gather(own_rows, ("dp", "tensor"), axis=0, tiled=True)
    contract = (((0,), (0,)), ((), ()))
    halves = [
        lax.dot_general(grads[k], xp, contract, preferred_element_type=jnp.float32) for k in (0, 1)
    ]
    summed = jnp.concatenate(halves, axis=1)
    return finish(summed, xp.shape[0], moment_m, moment_v)


def solution(mesh):
    return jax.shard_map(
        local,
        mesh=mesh,
        in_specs=(
            P(("dp", "tensor"), None),
            P("tensor", None),
            P("dp", "tensor"),
            P("dp", "tensor"),
            P("dp", "tensor"),
            P(("tensor", "dp"), None),
            P(("tensor", "dp"), None),
        ),
        out_specs=(P(("tensor", "dp"), None), P(("tensor", "dp"), None), P(("tensor", "dp"), None)),
        check_vma=False,
    )
```

time: 54.6 us -> 52.1 us (0.954)
  Pallas kernels: 53.7 us -> 50.8 us
    pallas_call x1, Pallas kernels: 50.9 us -> 48.2 us  [exchange(): pl.pallas_call(functools.partial(exchange_kernel, ndp, nt), out_shape=jax...]
where the time goes in v1:
time: 52.1 us; the launch traced here: 51.5 us
  Pallas kernels  50.8 us (98%)
  between operations  0.67 us (1%)
    pallas_call x1, Pallas kernels, exchange(): pl.pallas_call(functools.partial(exchange_kernel, ndp, nt), out_shape=jax...  48.2 us
    pallas_call x1, Pallas kernels, finish_call(): pl.pallas_call(functools.partial(finish_kernel, total_tokens, steps), out...  2.65 us

profile of v1, /device:TPU:9, one launch (start us, length us, event | category | flops | bytes accessed | tf_op | source)
XLA Modules:
  0.0 51.5 jit_solution(10063563594910059344)
XLA Ops:
  0.6 0.0 copy-start.1
  0.6 0.0 copy-start
  0.7 48.2 %shard_map.94.sum_ref = f32[480,1024]{1,0:T(8,128)S(1)} custom-call(bf16[32,8192]{1,0:T(8,128)(2,1)} %tok_ref.1, bf16[2048,512]{1,0:T(8,128)(2,1)} %prj_ref.1, bf16[128,3840]{1,0:T(8,128)(2,1)} %gate_ref.1, bf16[128,3840]{1,0:T(8,128)(2,1)} %up_ref.1, bf16[128,3840]{1,0:T(8,128)(2,1)} %hg_ref.1), custom_call_target="tpu_custom_call" | custom-call | flops 1275068416 | bytes 3932160 | tf_op jit(solution)/shard_map/pallas_call | solution.py:348
  48.8 0.0 copy-done.1
  48.8 0.0 copy-done
  48.9 2.7 %shard_map.95 = (f32[480,1024]{1,0:T(8,128)}, f32[480,1024]{1,0:T(8,128)}, f32[480,1024]{1,0:T(8,128)}) custom-call(f32[480,1024]{1,0:T(8,128)S(1)} %shard_map.94.sum_ref, f32[480,1024]{1,0:T(8,128)S(1)} %copy-done, f32[480,1024]{1,0:T(8,128)S(1)} %copy-done.1), custom_call_target="tpu_custom_call" | custom-call | tf_op jit(solution)/shard_map/pallas_call | solution.py:434
Async XLA Ops:
  0.6 48.2 %copy-start.1 = (f32[480,1024]{1,0:T(8,128)S(1)}, f32[480,1024]{1,0:T(8,128)}, u32[]{:S(2)}) copy-start(f32[480,1024]{1,0:T(8,128)} %v_ref.1) | copy-start | bytes 5898244
  0.6 48.2 %copy-start = (f32[480,1024]{1,0:T(8,128)S(1)}, f32[480,1024]{1,0:T(8,128)}, u32[]{:S(2)}) copy-start(f32[480,1024]{1,0:T(8,128)} %m_ref.1) | copy-start | bytes 5898244

commit v2 on v1

--- a/solution.py
+++ b/solution.py
@@ -10,12 +10,23 @@
 
 MESH = pl.DeviceIdType.MESH
 TAILS = 3
-OUTER_EARLY = ((1, 2, 0), (1, 0, 0), (0, 0, 1))
-OUTER = ((1, 3, 0), (1, 1, 0), (0, 1, 1), (1, 2, 1), (1, 0, 1), (1, 3, 1), (1, 1, 1))
-INNER_EARLY = ((0, 2, 0), (1, 0, 0), (1, 1, 0))
-EARLY_CUTS = ((0, 0),)
-INNER = ((0, 3, 0), (0, 2, 1), (0, 3, 1))
-OWN = ((1, 0, 1), (1, 1, 1))
+OUTER_EARLY = (
+    ((1, 2, 0), (1, 0, 0), (0, 0, 1)),
+    ((0, 0, 1), (1, 0, 0), (1, 2, 0)),
+)
+OUTER = (
+    ((1, 3, 0), (1, 1, 0), (0, 1, 1), (1, 2, 1), (1, 0, 1), (1, 3, 1), (1, 1, 1)),
+    ((0, 1, 1), (1, 1, 0), (1, 3, 0), (1, 0, 1), (1, 2, 1), (1, 1, 1), (1, 3, 1)),
+)
+INNER_EARLY = (
+    ((0, 2, 0), (1, 0, 0), (1, 1, 0), 0),
+    ((0, 3, 0), (1, 0, 0), (1, 1, 0), 0),
+)
+INNER = (
+    ((0, 3, 0), (1, 0, 1), (0, 2, 1), (0, 3, 1), 1, 2, 3, 4, 5),
+    ((0, 2, 0), (1, 0, 1), (0, 3, 1), (0, 2, 1), 1, 2, 3, 4, 5),
+)
+LATER = ((1, 1, 1),)
 def pieces(rows):
     cuts = [-(-rows * i // (16 * TAILS)) * 16 for i in range(TAILS)] + [rows]
     return list(zip(cuts, cuts[1:]))
@@ -25,7 +36,7 @@
     ndp, nt, tok_ref, prj_ref, gate_ref, up_ref, hg_ref, out_ref,
     acts, prj_v, cols, part, rs_buf, xp_all, grads, recv,
     load_sem, tok_send, tok_recv, rs_send, rs_recv,
-    xp_send, xz_recv, xt_recv, xc_recv, g_send, g_recv, cut_recv, late,
+    xp_send, xz_recv, xt_recv, xc_recv, g_send, g_recv, cut_recv, near, late,
 ):
     d = lax.axis_index("dp")
     t = lax.axis_index("tensor")
@@ -53,7 +64,7 @@
         return which * half + up * j + (1 - up) * (half - 1 - j)
 
     head = -(-rows // 128)
-    spans = ((first, 0, head), (first, head, half_tiles), (second, 0, half_tiles))
+    spans = ((first, 0, 1), (first, 1, half_tiles), (second, 0, half_tiles))
     loads, places = [], []
     for i, (which, start, stop) in enumerate(spans):
         low = which * half_tiles + up * start + (1 - up) * (half_tiles - stop)
@@ -87,8 +98,9 @@
     def _():
         greet(d + 1 - 2 * c, t)
 
+    host = inner * adj + (1 - inner) * z
     for k in range(1, nt):
-        greet(d, (t + k) % nt)
+        greet(host * 2 + c, (t + k) % nt)
 
     for load in loads[3:]:
         load.start()
@@ -161,23 +173,48 @@
     def send(which, j, side):
         grad_copy(dest_of(which, j), d, side).start()
 
-    def send_all(plan):
-        for part_of, j, side in plan:
-            send((first, second)[part_of], j, side)
-
-    def send_cuts(plan):
-        for p, j in plan:
-            cut_copy(dest_of(first, j), d, p).start()
+    def send_all(kind, plans):
+        for core, plan in enumerate(plans):
+
+            @pl.when((inner == kind) & (c == core))
+            def _():
+                for item in plan:
+                    if isinstance(item, int):
+                        cut_copy(dest_of(first, item % 2), d, item // 2).start()
+                    else:
+                        send((first, second)[item[0]], *item[1:])
 
     def need(j):
         return -(-((j + 1) * rows) // 128)
 
     drain(acts.at[:, :, places[0]], load_sem.at[0])
-    tiles_of(first, 0, head)
-    pl.semaphore_wait(barrier, nt - 1 + jnp.where(z == nz - 1, ndp - 1, ndp - 3))
-    send(first, 0, 0)
-    for k in range(1, nt):
-        tok_copy((t + k) % nt, t).start()
+    tiles_of(first, 0, 1)
+    known = jnp.where(z == nz - 1, ndp - 1, ndp - 3)
+    pl.semaphore_wait(barrier, known + (1 - inner) * 2 * (nt - 1))
+
+    def part_send(start, stop):
+        low = dest_of(first, 0) * rows + up * start + (1 - up) * (rows - stop)
+        at = pl.ds(pl.multiple_of(low, 16), stop - start)
+        back = up * start + (1 - up) * (rows - stop)
+        pltpu.make_async_remote_copy(
+            src_ref=grads.at[0, at, :],
+            dst_ref=recv.at[d, 0, pl.ds(pl.multiple_of(back, 16), stop - start), :],
+            send_sem=g_send.at[0],
+            recv_sem=g_recv.at[2 * z],
+            device_id=(dest_of(first, 0), t),
+            device_id_type=MESH,
+        ).start()
+
+    def send_tokens():
+        for k in range(1, nt):
+            tok_copy((t + k) % nt, t).start()
+
+    part_send(0, 128)
+
+    @pl.when(inner == 0)
+    def _():
+        pl.semaphore_signal(near, inc=1, device_id=(adj * 2 + c, t), device_id_type=MESH)
+        send_tokens()
 
     @pl.when(z == nz - 1)
     def _():
@@ -185,9 +222,17 @@
             pl.semaphore_signal(late, inc=1, device_id=(k, t), device_id_type=MESH)
 
     drain(acts.at[:, :, places[1]], load_sem.at[1])
+    tiles_of(first, 1, head)
+    part_send(128, rows)
     tiles_of(first, head, need(1))
     send(first, 1, 0)
     tiles_of(first, need(1), half_tiles)
+
+    @pl.when(inner == 1)
+    def _():
+        pl.semaphore_wait(near, 1)
+        send_tokens()
+
     drain(acts.at[:, :, places[2]], load_sem.at[2])
     tiles_of(second, 0, half_tiles)
 
@@ -195,14 +240,8 @@
     def _():
         pl.semaphore_wait(late, 2)
 
-    @pl.when(inner == 0)
-    def _():
-        send_all(OUTER_EARLY)
-
-    @pl.when(inner == 1)
-    def _():
-        send_all(INNER_EARLY)
-        send_cuts(EARLY_CUTS)
+    send_all(0, OUTER_EARLY)
+    send_all(1, INNER_EARLY)
 
     for j in (2, 3):
         for side in (0, 1):
@@ -251,14 +290,8 @@
     along_z(z, opp)
     along_z(z, adj)
 
-    @pl.when(inner == 0)
-    def _():
-        send_all(OUTER)
-
-    @pl.when(inner == 1)
-    def _():
-        send_all(INNER)
-        send_cuts([(p, j) for p in range(TAILS) for j in (0, 1) if (p, j) not in EARLY_CUTS])
+    send_all(0, OUTER)
+    send_all(1, INNER)
 
     order = [z, adj, far, opp]
 
@@ -271,9 +304,7 @@
         for kt in range(1, nt):
             piece_copy(dd, t, xt_recv.at[zz], (d, (t + kt) % nt)).start()
 
-    @pl.when(inner == 1)
-    def _():
-        send_all(OWN)
+    send_all(1, (LATER, LATER))
 
     partner = d + 1 - 2 * c
 
@@ -372,6 +403,7 @@
             dma((2 * nz,)),
             dma((TAILS,)),
             pltpu.SemaphoreType.REGULAR,
+            pltpu.SemaphoreType.REGULAR,
         ],
         compiler_params=pltpu.CompilerParams(
             collective_id=0, has_side_effects=True, vmem_limit_bytes=32 * 1024 * 1024

time: 52.1 us -> 51.4 us (0.987)
  Pallas kernels: 50.8 us -> 50.1 us
    pallas_call x1, Pallas kernels: 48.2 us -> 47.4 us  [exchange(): pl.pallas_call(functools.partial(exchange_kernel, ndp, nt), out_shape=jax...]
where the time goes in v2:
time: 51.4 us; the launch traced here: 50.8 us
  Pallas kernels  50.1 us (97%)
  between operations  0.67 us (1%)
    pallas_call x1, Pallas kernels, exchange(): pl.pallas_call(functools.partial(exchange_kernel, ndp, nt), out_shape=jax...  47.4 us
    pallas_call x1, Pallas kernels, finish_call(): pl.pallas_call(functools.partial(finish_kernel, total_tokens, steps), out...  2.65 us

profile of v2, /device:TPU:9, one launch (start us, length us, event | category | flops | bytes accessed | tf_op | source)
XLA Modules:
  0.0 50.8 jit_solution(10704583838912552872)
XLA Ops:
  0.6 0.0 copy-start.1
  0.6 0.0 copy-start
  0.7 47.4 %shard_map.94.sum_ref = f32[480,1024]{1,0:T(8,128)S(1)} custom-call(bf16[32,8192]{1,0:T(8,128)(2,1)} %tok_ref.1, bf16[2048,512]{1,0:T(8,128)(2,1)} %prj_ref.1, bf16[128,3840]{1,0:T(8,128)(2,1)} %gate_ref.1, bf16[128,3840]{1,0:T(8,128)(2,1)} %up_ref.1, bf16[128,3840]{1,0:T(8,128)(2,1)} %hg_ref.1), custom_call_target="tpu_custom_call" | custom-call | flops 1275068416 | bytes 3932160 | tf_op jit(solution)/shard_map/pallas_call | solution.py:379
  48.1 0.0 copy-done.1
  48.1 0.0 copy-done
  48.1 2.7 %shard_map.95 = (f32[480,1024]{1,0:T(8,128)}, f32[480,1024]{1,0:T(8,128)}, f32[480,1024]{1,0:T(8,128)}) custom-call(f32[480,1024]{1,0:T(8,128)S(1)} %shard_map.94.sum_ref, f32[480,1024]{1,0:T(8,128)S(1)} %copy-done, f32[480,1024]{1,0:T(8,128)S(1)} %copy-done.1), custom_call_target="tpu_custom_call" | custom-call | tf_op jit(solution)/shard_map/pallas_call | solution.py:466
Async XLA Ops:
  0.6 47.5 %copy-start.1 = (f32[480,1024]{1,0:T(8,128)S(1)}, f32[480,1024]{1,0:T(8,128)}, u32[]{:S(2)}) copy-start(f32[480,1024]{1,0:T(8,128)} %v_ref.1) | copy-start | bytes 5898244
  0.6 47.5 %copy-start = (f32[480,1024]{1,0:T(8,128)S(1)}, f32[480,1024]{1,0:T(8,128)}, u32[]{:S(2)}) copy-start(f32[480,1024]{1,0:T(8,128)} %m_ref.1) | copy-start | bytes 5898244

commit v3 on v2

--- a/solution.py
+++ b/solution.py
@@ -35,8 +35,8 @@
 def exchange_kernel(
     ndp, nt, tok_ref, prj_ref, gate_ref, up_ref, hg_ref, out_ref,
     acts, prj_v, cols, part, rs_buf, xp_all, grads, recv,
-    load_sem, tok_send, tok_recv, rs_send, rs_recv,
-    xp_send, xz_recv, xt_recv, xc_recv, g_send, g_recv, cut_recv, near, late,
+    load_sem, tok_recv, rs_recv, xp_send,
+    xz_recv, xt_recv, xc_recv, g_send, g_recv, cut_recv, near, late,
 ):
     d = lax.axis_index("dp")
     t = lax.axis_index("tensor")
@@ -64,15 +64,19 @@
         return which * half + up * j + (1 - up) * (half - 1 - j)
 
     head = -(-rows // 128)
-    spans = ((first, 0, 1), (first, 1, half_tiles), (second, 0, half_tiles))
+    spans = (
+        (first, 0, 1), (first, 1, head), (first, head, half_tiles), (second, 0, half_tiles)
+    )
     loads, places = [], []
     for i, (which, start, stop) in enumerate(spans):
         low = which * half_tiles + up * start + (1 - up) * (half_tiles - stop)
         at = pl.ds(pl.multiple_of(low * 128, 128), (stop - start) * 128)
         places.append(at)
         for k, src in enumerate((gate_ref, up_ref, hg_ref)):
-            loads.append(pltpu.make_async_copy(src.at[:, at], acts.at[k, :, at], load_sem.at[i]))
-    load_prj = pltpu.make_async_copy(prj_ref, prj_v, load_sem.at[3])
+            loads.append(
+                pltpu.make_async_copy(src.at[:, at], acts.at[k, :, at], load_sem.at[min(i, 2)])
+            )
+    load_prj = pltpu.make_async_copy(prj_ref, prj_v, load_sem.at[0])
     own_tok = pltpu.make_async_copy(
         tok_ref.at[:, pl.ds(pl.multiple_of(t * dcol, 128), dcol)],
         cols.at[pl.ds(pl.multiple_of(t * sub, 16), sub), :],
@@ -104,14 +108,13 @@
 
     for load in loads[3:]:
         load.start()
-    load_prj.start()
     own_tok.start()
 
     def tok_copy(dest, src):
         return pltpu.make_async_remote_copy(
             src_ref=tok_ref.at[:, pl.ds(pl.multiple_of(dest * dcol, 128), dcol)],
             dst_ref=cols.at[pl.ds(pl.multiple_of(src * sub, 16), sub), :],
-            send_sem=tok_send.at[0],
+            send_sem=xp_send.at[0],
             recv_sem=tok_recv.at[0],
             device_id=(d, dest),
             device_id_type=MESH,
@@ -141,7 +144,7 @@
             src_ref=block_of(dest, side),
             dst_ref=recv.at[src, side],
             send_sem=g_send.at[0],
-            recv_sem=g_recv.at[src // 2 * 2 + side],
+            recv_sem=g_recv.at[src // 2],
             device_id=(dest, t),
             device_id_type=MESH,
         )
@@ -159,7 +162,7 @@
         )
 
     def own_grad(side):
-        return pltpu.make_async_copy(block_of(d, side), recv.at[d, side], g_recv.at[2 * z + side])
+        return pltpu.make_async_copy(block_of(d, side), recv.at[d, side], g_recv.at[z])
 
     def send_near(dest, side):
         @pl.when(dest != d)
@@ -188,6 +191,7 @@
         return -(-((j + 1) * rows) // 128)
 
     drain(acts.at[:, :, places[0]], load_sem.at[0])
+    load_prj.start()
     tiles_of(first, 0, 1)
     known = jnp.where(z == nz - 1, ndp - 1, ndp - 3)
     pl.semaphore_wait(barrier, known + (1 - inner) * 2 * (nt - 1))
@@ -200,7 +204,7 @@
             src_ref=grads.at[0, at, :],
             dst_ref=recv.at[d, 0, pl.ds(pl.multiple_of(back, 16), stop - start), :],
             send_sem=g_send.at[0],
-            recv_sem=g_recv.at[2 * z],
+            recv_sem=g_recv.at[z],
             device_id=(dest_of(first, 0), t),
             device_id_type=MESH,
         ).start()
@@ -224,6 +228,7 @@
     drain(acts.at[:, :, places[1]], load_sem.at[1])
     tiles_of(first, 1, head)
     part_send(128, rows)
+    drain(acts.at[:, :, : (2 * half_tiles - head) * 128], load_sem.at[2])
     tiles_of(first, head, need(1))
     send(first, 1, 0)
     tiles_of(first, need(1), half_tiles)
@@ -233,7 +238,6 @@
         pl.semaphore_wait(near, 1)
         send_tokens()
 
-    drain(acts.at[:, :, places[2]], load_sem.at[2])
     tiles_of(second, 0, half_tiles)
 
     @pl.when(z < nz - 1)
@@ -249,13 +253,14 @@
 
     load_prj.wait()
     drain(cols, tok_recv.at[0])
+    drain(cols.at[: (nt - 1) * sub, :], xp_send.at[0])
     part[...] = jnp.dot(cols[...], prj_v[...], preferred_element_type=jnp.float32)
 
     def rs_copy(dest, src):
         return pltpu.make_async_remote_copy(
             src_ref=part.at[pl.ds(pl.multiple_of(dest * sub, 16), sub), :],
             dst_ref=rs_buf.at[src],
-            send_sem=rs_send.at[0],
+            send_sem=xp_send.at[0],
             recv_sem=rs_recv.at[0],
             device_id=(d, dest),
             device_id_type=MESH,
@@ -265,6 +270,7 @@
         rs_copy((t + k) % nt, t).start()
     rs_buf[t] = part[pl.ds(pl.multiple_of(t * sub, 16), sub), :]
     drain(rs_buf.at[: nt - 1], rs_recv.at[0])
+    drain(rs_buf.at[: nt - 1], xp_send.at[0])
     total = rs_buf[0]
     for k in range(1, nt):
         total = total + rs_buf[k]
@@ -284,11 +290,11 @@
             device_id_type=MESH,
         )
 
-    def along_z(zz, dest):
-        piece_copy(zz * 2 + c, t, xz_recv.at[zz], (dest * 2 + c, t)).start()
-
-    along_z(z, opp)
-    along_z(z, adj)
+    def along_z(zz, dest, slot):
+        piece_copy(zz * 2 + c, t, xz_recv.at[slot], (dest * 2 + c, t)).start()
+
+    along_z(z, opp, 1 + inner)
+    along_z(z, adj, 0)
 
     send_all(0, OUTER)
     send_all(1, INNER)
@@ -298,30 +304,31 @@
     for k, zz in enumerate(order):
         dd = zz * 2 + c
         if k:
-            drain(piece(dd, t), xz_recv.at[zz])
+            drain(piece(dd, t), xz_recv.at[k - 1])
         if k > 1:
-            pl.when(inner == 1)(functools.partial(along_z, zz, adj))
+            pl.when(inner == 1)(functools.partial(along_z, zz, adj, k - 1))
         for kt in range(1, nt):
-            piece_copy(dd, t, xt_recv.at[zz], (d, (t + kt) % nt)).start()
+            piece_copy(dd, t, xt_recv.at[k // 2], (d, (t + kt) % nt)).start()
 
     send_all(1, (LATER, LATER))
 
     partner = d + 1 - 2 * c
 
-    def core_copy(zz, parity):
+    def core_copy(zz, parity, slot):
         group = xp_all.at[pl.ds(pl.multiple_of((zz * 2 + parity) * grp, 128), grp), :]
         return pltpu.make_async_remote_copy(
             src_ref=group,
             dst_ref=group,
             send_sem=xp_send.at[0],
-            recv_sem=xc_recv.at[zz],
+            recv_sem=xc_recv.at[slot],
             device_id=(partner, t),
             device_id_type=MESH,
         )
 
-    for zz in order:
-        drain(xp_all.at[: (nt - 1) * sub, :], xt_recv.at[zz])
-        core_copy(zz, c).start()
+    for slot in (0, 1):
+        drain(xp_all.at[: 2 * (nt - 1) * sub, :], xt_recv.at[slot])
+        for zz in order[2 * slot : 2 * slot + 2]:
+            core_copy(zz, c, slot).start()
 
     def add_term(k, zz, side, low, count):
         at = pl.ds(low, count)
@@ -334,31 +341,29 @@
         else:
             out_ref[at, cols_at] += term
 
-    def take(k, zz, side):
-        drain(recv.at[pl.ds(zz * 2, 2), side], g_recv.at[2 * zz + side])
-        add_term(k, zz, side, 0, rows)
-
-    for k in (0, 1):
-        core_copy(order[k], 1 - c).wait_recv()
+    def take(k, zz):
+        drain(recv.at[pl.ds(zz * 2, 2)], g_recv.at[zz])
         for side in (0, 1):
-            take(k, order[k], side)
-    core_copy(far, 1 - c).wait_recv()
-    core_copy(opp, 1 - c).wait_recv()
-    drain(cols.at[: (nt - 1) * sub, :], tok_send.at[0])
-    drain(rs_buf.at[: nt - 1], rs_send.at[0])
+            add_term(k, zz, side, 0, rows)
+
+    groups = xp_all.at[: 2 * grp, :]
+    drain(groups, xc_recv.at[0])
+    take(0, z)
+    take(1, adj)
+    drain(groups, xc_recv.at[1])
     moved = (nt - 1) * nz + nt * nz + 2
     pl.when(inner == 0)(lambda: drain(xp_all.at[: moved * sub, :], xp_send.at[0]))
     pl.when(inner == 1)(lambda: drain(xp_all.at[: (moved + 2) * sub, :], xp_send.at[0]))
-    take(3, opp, 0)
-    take(2, far, 0)
-    take(2, far, 1)
+    take(2, far)
 
     @pl.when(inner == 0)
     def _():
-        take(3, opp, 1)
+        take(3, opp)
 
     @pl.when(inner == 1)
     def _():
+        drain(recv.at[pl.ds(opp * 2, 2), 0], g_recv.at[opp])
+        add_term(3, opp, 0, 0, rows)
         for p, (start, stop) in enumerate(cut):
             drain(recv.at[pl.ds(opp * 2, 2), 1, start:stop, :], cut_recv.at[p])
             add_term(3, opp, 1, start, stop - start)
@@ -390,17 +395,15 @@
             pltpu.VMEM((grp * ndp, rank), bf),
             pltpu.VMEM((2, cols, grp), bf),
             pltpu.VMEM((ndp, 2, rows, grp), bf),
-            dma((4,)),
+            dma((3,)),
             dma((1,)),
             dma((1,)),
             dma((1,)),
-            dma((1,)),
+            dma((3,)),
+            dma((2,)),
+            dma((2,)),
             dma((1,)),
             dma((nz,)),
-            dma((nz,)),
-            dma((nz,)),
-            dma((1,)),
-            dma((2 * nz,)),
             dma((TAILS,)),
             pltpu.SemaphoreType.REGULAR,
             pltpu.SemaphoreType.REGULAR,

time: 51.4 us -> 51 us (level)
  no operation moved by 1% of the time
where the time goes in v3:
time: 51 us; the launch traced here: 50.4 us
  Pallas kernels  49.7 us (97%)
  between operations  0.67 us (1%)
    pallas_call x1, Pallas kernels, exchange(): pl.pallas_call(functools.partial(exchange_kernel, ndp, nt), out_shape=jax...  47.1 us
    pallas_call x1, Pallas kernels, finish_call(): pl.pallas_call(functools.partial(finish_kernel, total_tokens, steps), out...  2.65 us

profile of v3, /device:TPU:9, one launch (start us, length us, event | category | flops | bytes accessed | tf_op | source)
XLA Modules:
  0.0 50.4 jit_solution(6989579549978202172)
XLA Ops:
  0.6 0.0 copy-start.1
  0.6 0.0 copy-start
  0.7 47.1 %shard_map.94.sum_ref = f32[480,1024]{1,0:T(8,128)S(1)} custom-call(bf16[32,8192]{1,0:T(8,128)(2,1)} %tok_ref.1, bf16[2048,512]{1,0:T(8,128)(2,1)} %prj_ref.1, bf16[128,3840]{1,0:T(8,128)(2,1)} %gate_ref.1, bf16[128,3840]{1,0:T(8,128)(2,1)} %up_ref.1, bf16[128,3840]{1,0:T(8,128)(2,1)} %hg_ref.1), custom_call_target="tpu_custom_call" | custom-call | flops 1275068416 | bytes 3932160 | tf_op jit(solution)/shard_map/pallas_call | solution.py:384
  47.7 0.0 copy-done.1
  47.7 0.0 copy-done
  47.8 2.7 %shard_map.95 = (f32[480,1024]{1,0:T(8,128)}, f32[480,1024]{1,0:T(8,128)}, f32[480,1024]{1,0:T(8,128)}) custom-call(f32[480,1024]{1,0:T(8,128)S(1)} %shard_map.94.sum_ref, f32[480,1024]{1,0:T(8,128)S(1)} %copy-done, f32[480,1024]{1,0:T(8,128)S(1)} %copy-done.1), custom_call_target="tpu_custom_call" | custom-call | tf_op jit(solution)/shard_map/pallas_call | solution.py:469
Async XLA Ops:
  0.6 47.1 %copy-start.1 = (f32[480,1024]{1,0:T(8,128)S(1)}, f32[480,1024]{1,0:T(8,128)}, u32[]{:S(2)}) copy-start(f32[480,1024]{1,0:T(8,128)} %v_ref.1) | copy-start | bytes 5898244
  0.6 47.1 %copy-start = (f32[480,1024]{1,0:T(8,128)S(1)}, f32[480,1024]{1,0:T(8,128)}, u32[]{:S(2)}) copy-start(f32[480,1024]{1,0:T(8,128)} %m_ref.1) | copy-start | bytes 5898244

commit v4 on v3

--- a/solution.py
+++ b/solution.py
@@ -33,7 +33,7 @@
 
 
 def exchange_kernel(
-    ndp, nt, tok_ref, prj_ref, gate_ref, up_ref, hg_ref, out_ref,
+    ndp, nt, tok_ref, prj_ref, gate_ref, up_ref, hg_ref, m_ref, v_ref, out_ref, m_out, v_out,
     acts, prj_v, cols, part, rs_buf, xp_all, grads, recv,
     load_sem, tok_recv, rs_recv, xp_send,
     xz_recv, xt_recv, xc_recv, g_send, g_recv, cut_recv, near, late,
@@ -252,6 +252,12 @@
             send_near(dest_of(own_half, j), side)
 
     load_prj.wait()
+    moments = [
+        pltpu.make_async_copy(m_ref, m_out, load_sem.at[1]),
+        pltpu.make_async_copy(v_ref, v_out, load_sem.at[2]),
+    ]
+    for load in moments:
+        load.start()
     drain(cols, tok_recv.at[0])
     drain(cols.at[: (nt - 1) * sub, :], xp_send.at[0])
     part[...] = jnp.dot(cols[...], prj_v[...], preferred_element_type=jnp.float32)
@@ -351,6 +357,8 @@
     take(0, z)
     take(1, adj)
     drain(groups, xc_recv.at[1])
+    for load in moments:
+        load.wait()
     moved = (nt - 1) * nz + nt * nz + 2
     pl.when(inner == 0)(lambda: drain(xp_all.at[: moved * sub, :], xp_send.at[0]))
     pl.when(inner == 1)(lambda: drain(xp_all.at[: (moved + 2) * sub, :], xp_send.at[0]))
@@ -371,7 +379,7 @@
     drain(recv.at[: ndp - 1], g_send.at[0])
 
 
-def exchange(ndp, nt, tokens_in, projector, gate_pre, up_pre, hidden_grad):
+def exchange(ndp, nt, tokens_in, projector, gate_pre, up_pre, hidden_grad, moment_m, moment_v):
     sub, width = tokens_in.shape
     depth, rank = projector.shape
     grp, cols = gate_pre.shape
@@ -379,13 +387,13 @@
     dma = pltpu.SemaphoreType.DMA
     bf, f32 = jnp.bfloat16, jnp.float32
     nz = ndp // 2
-    operands = (tokens_in, projector, gate_pre, up_pre, hidden_grad)
+    operands = (tokens_in, projector, gate_pre, up_pre, hidden_grad, moment_m, moment_v)
     flops = 2 * grp * depth * rank + 4 * rows * grp * ndp * rank
     return pl.pallas_call(
         functools.partial(exchange_kernel, ndp, nt),
-        out_shape=jax.ShapeDtypeStruct((rows, 2 * rank), f32),
-        in_specs=[pl.BlockSpec(memory_space=pltpu.HBM)] * 5,
-        out_specs=pl.BlockSpec(memory_space=pltpu.VMEM),
+        out_shape=(jax.ShapeDtypeStruct((rows, 2 * rank), f32),) * 3,
+        in_specs=[pl.BlockSpec(memory_space=pltpu.HBM)] * 7,
+        out_specs=(pl.BlockSpec(memory_space=pltpu.VMEM),) * 3,
         scratch_shapes=[
             pltpu.VMEM((3, grp, cols), bf),
             pltpu.VMEM((depth, rank), bf),
@@ -463,7 +471,7 @@
         pltpu.make_async_copy(bufs[k], outs[k], sem.at[k]).wait()
 
 
-def finish_call(summed, total_tokens, moment_m, moment_v):
+def finish_call(summed, moment_m, moment_v, total_tokens):
     steps = 6
     shape = jax.ShapeDtypeStruct(summed.shape, jnp.float32)
     return pl.pallas_call(
@@ -480,8 +488,8 @@
 def local(tokens_in, projector, gate_pre, up_pre, hidden_grad, moment_m, moment_v):
     ndp, nt = lax.axis_size("dp"), lax.axis_size("tensor")
     if fits(ndp, nt, tokens_in, projector, gate_pre):
-        summed = exchange(ndp, nt, tokens_in, projector, gate_pre, up_pre, hidden_grad)
-        return tuple(finish_call(summed, gate_pre.shape[0] * ndp, moment_m, moment_v))
+        operands = tokens_in, projector, gate_pre, up_pre, hidden_grad, moment_m, moment_v
+        return tuple(finish_call(*exchange(ndp, nt, *operands), gate_pre.shape[0] * ndp))
     gate = gate_pre.astype(jnp.float32)
     hgrad = hidden_grad.astype(jnp.float32)
     sig = jax.nn.sigmoid(gate)

time: 51 us -> 50.9 us (level)
  no operation moved by 1% of the time
where the time goes in v4:
time: 50.9 us; the launch traced here: 50.2 us
  Pallas kernels  49.6 us (97%)
  between operations  0.64 us (1%)
    pallas_call x1, Pallas kernels, exchange(): pl.pallas_call(functools.partial(exchange_kernel, ndp, nt), out_shape=(ja...  47 us
    pallas_call x1, Pallas kernels, finish_call(): pl.pallas_call(functools.partial(finish_kernel, total_tokens, steps), out...  2.65 us

profile of v4, /device:TPU:9, one launch (start us, length us, event | category | flops | bytes accessed | tf_op | source)
XLA Modules:
  0.0 50.2 jit_solution(2634719115459804243)
XLA Ops:
  0.6 47.0 %shard_map.94 = (f32[480,1024]{1,0:T(8,128)S(1)}, f32[480,1024]{1,0:T(8,128)S(1)}, f32[480,1024]{1,0:T(8,128)S(1)}) custom-call(bf16[32,8192]{1,0:T(8,128)(2,1)} %tok_ref.1, bf16[2048,512]{1,0:T(8,128)(2,1)} %prj_ref.1, bf16[128,3840]{1,0:T(8,128)(2,1)} %gate_ref.1, bf16[128,3840]{1,0:T(8,128)(2,1)} %up_ref.1, bf16[128,3840]{1,0:T(8,128)(2,1)} %hg_ref.1, ...), custom_call_target="tpu_custom_call" | custom-call | flops 1275068416 | bytes 3932160 | tf_op jit(solution)/shard_map/pallas_call | solution.py:392
  47.6 2.7 %shard_map.95 = (f32[480,1024]{1,0:T(8,128)}, f32[480,1024]{1,0:T(8,128)}, f32[480,1024]{1,0:T(8,128)}) custom-call(f32[480,1024]{1,0:T(8,128)S(1)} %get-tuple-element.6.sum_ref, f32[480,1024]{1,0:T(8,128)S(1)} %get-tuple-element.7.m_ref, f32[480,1024]{1,0:T(8,128)S(1)} %get-tuple-element.8.v_ref), custom_call_target="tpu_custom_call" | custom-call | tf_op jit(solution)/shard_map/pallas_call | solution.py:477

commit v5 on v4

--- a/solution.py
+++ b/solution.py
@@ -455,11 +455,11 @@
     return (m_next, v_next, direction)
 
 
-def finish_kernel(total_tokens, steps, sum_ref, m_ref, v_ref, *refs):
+def finish_kernel(total_tokens, sum_ref, m_ref, v_ref, *refs):
     outs, bufs, sem = refs[:3], refs[3:6], refs[6]
-    rows = sum_ref.shape[0] // steps
-    for i in range(steps):
-        at = slice(i * rows, (i + 1) * rows)
+    rows = sum_ref.shape[0]
+    cuts = [0] + [-(-rows * k // 80) * 8 for k in (1, 2, 4, 6, 8)] + [rows]
+    for at in map(slice, cuts, cuts[1:]):
         values = finish(sum_ref[at, :], total_tokens, m_ref[at, :], v_ref[at, :])
         for k in range(3):
             bufs[k][at, :] = values[k]
@@ -472,10 +472,9 @@
 
 
 def finish_call(summed, moment_m, moment_v, total_tokens):
-    steps = 6
     shape = jax.ShapeDtypeStruct(summed.shape, jnp.float32)
     return pl.pallas_call(
-        functools.partial(finish_kernel, total_tokens, steps),
+        functools.partial(finish_kernel, total_tokens),
         out_shape=(shape,) * 3,
         in_specs=[pl.BlockSpec(memory_space=pltpu.VMEM)] * 3,
         out_specs=[pl.BlockSpec(memory_space=pltpu.HBM)] * 3,

time: 50.9 us -> 50.8 us (level)
  no operation moved by 1% of the time
where the time goes in v5:
time: 50.8 us; the launch traced here: 50.2 us
  Pallas kernels  49.6 us (98%)
  between operations  0.64 us (1%)
    pallas_call x1, Pallas kernels, exchange(): pl.pallas_call(functools.partial(exchange_kernel, ndp, nt), out_shape=(ja...  47 us
    pallas_call x1, Pallas kernels, finish_call(): pl.pallas_call(functools.partial(finish_kernel, total_tokens), out_shape=...  2.61 us

profile of v5, /device:TPU:9, one launch (start us, length us, event | category | flops | bytes accessed | tf_op | source)
XLA Modules:
  0.0 50.2 jit_solution(9161033962023088813)
XLA Ops:
  0.6 47.0 %shard_map.94 = (f32[480,1024]{1,0:T(8,128)S(1)}, f32[480,1024]{1,0:T(8,128)S(1)}, f32[480,1024]{1,0:T(8,128)S(1)}) custom-call(bf16[32,8192]{1,0:T(8,128)(2,1)} %tok_ref.1, bf16[2048,512]{1,0:T(8,128)(2,1)} %prj_ref.1, bf16[128,3840]{1,0:T(8,128)(2,1)} %gate_ref.1, bf16[128,3840]{1,0:T(8,128)(2,1)} %up_ref.1, bf16[128,3840]{1,0:T(8,128)(2,1)} %hg_ref.1, ...), custom_call_target="tpu_custom_call" | custom-call | flops 1275068416 | bytes 3932160 | tf_op jit(solution)/shard_map/pallas_call | solution.py:392
  47.6 2.6 %shard_map.95 = (f32[480,1024]{1,0:T(8,128)}, f32[480,1024]{1,0:T(8,128)}, f32[480,1024]{1,0:T(8,128)}) custom-call(f32[480,1024]{1,0:T(8,128)S(1)} %get-tuple-element.6.sum_ref, f32[480,1024]{1,0:T(8,128)S(1)} %get-tuple-element.7.m_ref, f32[480,1024]{1,0:T(8,128)S(1)} %get-tuple-element.8.v_ref), custom_call_target="tpu_custom_call" | custom-call | tf_op jit(solution)/shard_map/pallas_call | solution.py:476
